TPU v7x, 256 devices: a whole 4x4x8 slice. The times are simulated.
256 devices in a mesh: video: 4 (over x), tm: 16 (over z, core), space: 4 (over y).
Axes of the slice: x: 4, y: 4, z: 8, core: 2. Of those that a mesh axis runs over, the one named last changes fastest.
Arguments:
- feature_maps: bfloat16 [64, 128, 240, 128], P(('video', 'tm'), 'space'), parts along dimension 0, may hold values from -27 to 27
- query_frame: int32 [2048], P('video'), parts along dimension 0, may hold values from 0 to 15
- query_row: int32 [2048], P('video'), parts along dimension 0, may hold values from 0 to 127
- query_col: int32 [2048], P('video'), parts along dimension 0, may hold values from 0 to 239
- ema_decay: float32 [64, 128], P(('video', 'tm')), parts along dimension 0, may hold values from 0.14 to 1
- dw_kernel: float32 [3, 128], replicated, may hold values from -3 to 3
- pw_weight: bfloat16 [128, 128], replicated, may hold values from -0.5 to 0.5
- out_weight: float32 [2, 128], replicated, may hold values from -2 to 2
Outputs:
- tracks: float32 [64, 2, 512], P(('video', 'tm')), parts along dimension 0
There are 4 independent parts, one for each index of `video`. A program takes and returns all parts, laid end to end along the dimension named above; an argument that names none is the same for every part. Nothing has to cross between parts.
All inputs are finite; a program needn't handle non-finite values.
Results may differ from a plain program's by a relative error of at most 0.0026.
Values may be sent and summed in bfloat16 or wider, within the bound.
A program may use at most 128 MiB of HBM per device.

v0:
```python
import math
import jax
import jax.numpy as jnp
from jax import lax
from jax.sharding import PartitionSpec as P


def with_halo(cells, sides, width):
    for axis, dim in sides:
        count = lax.axis_size(axis)
        ends = count - 1
        head = lax.slice_in_dim(cells, 0, width, axis=dim)
        tail = lax.slice_in_dim(cells, cells.shape[dim] - width, cells.shape[dim], axis=dim)
        cells = jnp.concatenate(
            [
                lax.ppermute(tail, axis, [(i, (i + 1) % count) for i in range(ends)]),
                cells,
                lax.ppermute(head, axis, [((i + 1) % count, i) for i in range(ends)]),
            ],
            axis=dim,
        )
    return cells


def local(
    feature_maps, query_frame, query_row, query_col, ema_decay, dw_kernel, pw_weight, out_weight
):
    frames_here, rows_here, map_width, channels = feature_maps.shape
    num_queries = query_frame.shape[0]
    first_frame = lax.axis_index("tm") * frames_here
    first_row = lax.axis_index("space") * rows_here
    map_height = rows_here * lax.axis_size("space")
    local_frame = query_frame - first_frame
    local_row = query_row - first_row
    owned = (
        (local_frame >= 0)
        & (local_frame < frames_here)
        & (local_row >= 0)
        & (local_row < rows_here)
    )
    picked = feature_maps[
        jnp.clip(local_frame, 0, frames_here - 1), jnp.clip(local_row, 0, rows_here - 1), query_col
    ]
    contrib = jnp.where(owned[:, None], picked.astype(jnp.float32), 0.0)
    query_feats = lax.psum(contrib, ("tm", "space")).astype(jnp.bfloat16)
    scale = 1.0 / math.sqrt(channels)
    col_coord = jnp.arange(map_width, dtype=jnp.int32).astype(jnp.float32) / map_width
    row_coord = (first_row + jnp.arange(rows_here, dtype=jnp.int32)).astype(
        jnp.float32
    ) / map_height
    highest_list, total_list, pos_list, feat_list = ([], [], [], [])
    frame_index = 0
    frame_map = feature_maps[frame_index].reshape(rows_here * map_width, channels)
    scores = (
        lax.dot_general(
            query_feats, frame_map, (((1,), (1,)), ((), ())), preferred_element_type=jnp.float32
        )
        * scale
    )
    highest = jnp.max(scores, axis=1)
    weights_exp = jnp.exp(scores - highest[:, None])
    highest_list.append(highest)
    total_list.append(jnp.sum(weights_exp, axis=1))
    grid = weights_exp.reshape(num_queries, rows_here, map_width)
    col_part = jnp.sum(jnp.sum(grid, axis=1) * col_coord[None, :], axis=1)
    line_portion = jnp.sum(jnp.sum(grid, axis=2) * row_coord[None, :], axis=1)
    pos_list.append(jnp.stack([col_part, line_portion], 1))
    feat_list.append(
        jnp.dot(weights_exp.astype(jnp.bfloat16), frame_map, preferred_element_type=jnp.float32)
    )
    highest = jnp.stack(highest_list)
    totals = jnp.stack(total_list)
    pos_sum = jnp.stack(pos_list)
    feat_sum = jnp.stack(feat_list)
    top_value = lax.pmax(highest, "space")
    factor = jnp.exp(highest - top_value)
    grand_total, pos_all, feat_all = lax.psum(
        (factor * totals, factor[..., None] * pos_sum, factor[..., None] * feat_sum), "space"
    )
    position = pos_all / grand_total[..., None]
    focused_result = (feat_all / grand_total[..., None]).astype(jnp.bfloat16)
    padded = with_halo(focused_result, (("tm", 0),), 1).astype(jnp.float32)
    depth = jnp.zeros((frames_here, num_queries, channels), jnp.float32)
    for tap in range(dw_kernel.shape[0]):
        depth = depth + dw_kernel[tap][None, None, :] * padded[tap : tap + frames_here]
    hidden = jax.nn.gelu(depth).astype(jnp.bfloat16)
    mixed = jnp.dot(
        hidden.reshape(-1, channels), pw_weight, preferred_element_type=jnp.float32
    ).reshape(frames_here, num_queries, channels)
    refined = focused_result.astype(jnp.float32) + mixed
    carried = jnp.zeros((num_queries, channels), jnp.float32)
    retain_prod = jnp.ones((channels,), jnp.float32)
    local_states, local_prods = ([], [])
    frame_index = 0
    retain = ema_decay[frame_index]
    carried = retain[None, :] * carried + (1.0 - retain[None, :]) * refined[frame_index]
    retain_prod = retain_prod * retain
    local_states.append(carried)
    local_prods.append(retain_prod)
    all_prods, all_ends = (
        lax.all_gather(retain_prod[None], "tm", axis=0, tiled=True),
        lax.all_gather(carried[None], "tm", axis=0, tiled=True),
    )
    position_tm = lax.axis_index("tm")

    def fold_step(source, running):
        advanced = all_prods[source][None, :] * running + all_ends[source]
        return jnp.where(source < position_tm, advanced, running)

    incoming = lax.fori_loop(
        0, lax.axis_size("tm"), fold_step, jnp.zeros((num_queries, channels), jnp.float32)
    )
    memory = jnp.stack(local_states) + jnp.stack(local_prods)[:, None, :] * incoming[None]
    delta = jnp.einsum("tqc,kc->tkq", memory, out_weight, precision=lax.Precision.HIGHEST)
    return jnp.transpose(position, (0, 2, 1)) + delta


def solution(mesh):
    placed = (
        P(("video", "tm"), "space", None, None),
        P("video"),
        P("video"),
        P("video"),
        P(("video", "tm"), None),
        P(),
        P(),
        P(),
    )
    return jax.shard_map(
        local, mesh=mesh, in_specs=placed, out_specs=P(("video", "tm"), None, None), check_vma=False
    )
```

profile of v0, /device:TPU:1, one launch (start us, length us, event | category | flops | bytes accessed | tf_op | source)
XLA Modules:
  0.0 416.0 jit_solution(9454271297745757524)
XLA Ops:
  8.1 3.1 gather_fusion
  11.4 250.4 %all-reduce.5 = bf16[512,128]{1,0:T(8,128)(2,1)S(1)} all-reduce(f32[512,128]{1,0:T(8,128)S(1)} %convert_select_fusion), channel_id=1, replica_groups=mesh['video'=4,'tm'=16,'space'=4] {'tm','space'}, use_global_device_ids=true, to_apply=%region_0.1 | all-reduce | flops 65536 | bytes 393216 | tf_op jit(solution)/shard_map/psum | solution.py:45
  261.8 2.3 multiply_reduce_fusion
  264.1 7.0 %fusion.50 = (f32[512]{0:T(512)S(1)}, f32[512,7680]{1,0:T(8,128)}) fusion(f32[512]{0:T(512)S(1)} %get-tuple-element.139, f32[512,7680]{1,0:T(8,128)S(1)} %get-tuple-element.140), kind=kLoop, calls=%fused_computation.74 | loop fusion | flops 11795968 | bytes 31461376 | tf_op jit(solution)/shard_map/reduce_sum | solution.py:63
  271.1 6.0 %pmax.7 = f32[1,512]{1,0:T(1,128)S(1)} all-reduce(f32[1,512]{1,0:T(1,128)S(1)} %bitcast.66), channel_id=1, replica_groups=mesh['video'=4,'tm'=16,'space'=4] {'space'}, use_global_device_ids=true, to_apply=%region_2.3 | all-reduce | flops 512 | bytes 4096 | tf_op jit(solution)/shard_map/pmax | solution.py:75
  277.1 8.4 %fusion.7 = f32[1,512,128]{2,1,0:T(8,128)} fusion(bf16[7680,128]{1,0:T(8,128)(2,1)S(1)} %bitcast.62, f32[512,7680]{1,0:T(8,128)} %get-tuple-element.135, f32[512]{0:T(512)S(1)} %bitcast.64), kind=kOutput, calls=%fused_computation.11 | convolution fusion | flops 1010630656 | bytes 17958912 | tf_op jit(solution)/shard_map/dot_general | solution.py:69
  285.5 15.7 %copy.10 = f32[512,7680]{0,1:T(8,128)} copy(f32[512,7680]{1,0:T(8,128)} %get-tuple-element.135) | data formatting | bytes 31457280 | tf_op jit(solution)/shard_map/exp | solution.py:61
  301.3 7.9 %fusion.48 = (f32[512,240]{0,1:T(8,128)S(1)}, f32[512,32]{0,1:T(8,128)S(1)}) fusion(f32[512,32,240]{0,2,1:T(8,128)} %bitcast.63), kind=kLoop, calls=%fused_computation.72 | loop fusion | flops 7725056 | bytes 16285696 | tf_op jit(solution)/shard_map/reduce_sum | solution.py:65
  309.4 7.5 %all-reduce = (f32[512]{0:T(512)S(1)}, f32[1,512,2]{1,2,0:T(2,128)S(1)}) all-reduce(f32[512]{0:T(512)S(1)} %bitcast.70, f32[1,512,2]{1,2,0:T(2,128)S(1)} %maximum_multiply_fusion), channel_id=1, replica_groups=mesh['video'=4,'tm'=16,'space'=4] {'space'}, use_global_device_ids=true, to_apply=%region_9.10 | all-reduce | flops 1536 | bytes 12288 | tf_op jit(solution)/shard_map/psum | solution.py:77
  317.0 15.6 %all-reduce.4.cloned.1.call-done = f32[1,512,128]{2,1,0:T(8,128)} async-done(((f32[1,512,128]{2,1,0:T(8,128)}), f32[1,512,128]{2,1,0:T(8,128)}) %all-reduce.4.cloned.1.call-update) | async-done | bytes 262160 | tf_op jit(solution)/shard_map/psum | solution.py:77
  333.7 4.7 %collective-permute-start.1 = (bf16[1,512,128]{2,1,0:T(8,128)(2,1)S(1)}, bf16[1,512,128]{2,1,0:T(8,128)(2,1)S(1)}, u32[]{:S(2)}, u32[]{:S(2)}) collective-permute-start(bf16[1,512,128]{2,1,0:T(8,128)(2,1)S(1)} %divide_convert_fusion), channel_id=1, source_target_pairs={{4,0},{8,4},{12,8},{16,12},{20,16},{24,20},{28,24},{32,28},{36,32}... | collective-permute-start | bytes 393224 | tf_op jit(solution)/shard_map/ppermute | solution.py:18
  338.4 3.1 collective-permute-start
  342.2 1.2 collective-permute-done
  344.5 18.6 %all-gather = f32[16,1,128]{2,1,0:T(1,128)S(1)} all-gather(f32[1,1,128]{2,1,0:T(1,128)S(1)} %bitcast.73), channel_id=1, replica_groups=mesh['video'=4,'tm'=16,'space'=4] {'tm'}, dimensions={0}, use_global_device_ids=true | all-gather | bytes 8704 | tf_op jit(solution)/shard_map/all_gather | solution.py:101
  363.0 26.2 %all-gather.3.cloned.1.call-done = f32[16,512,128]{2,1,0:T(8,128)} async-done(((f32[1,512,128]{2,1,0:T(8,128)}), f32[16,512,128]{2,1,0:T(8,128)}) %all-gather.3.cloned.1.call-update) | async-done | bytes 4194320 | tf_op jit(solution)/shard_map/all_gather | solution.py:102
  389.2 19.0 %while.14 = (s32[]{:T(128)}, f32[512,128]{1,0:T(8,128)S(1)}, s32[]{:T(128)}, f32[16,128]{1,0:T(8,128)S(1)}, f32[16,512,128]{2,1,0:T(8,128)}, /*index=5*/s32[]{:T(128)}, s32[]{:T(128)}) while((s32[]{:T(128)}, f32[512,128]{1,0:T(8,128)S(1)}, s32[]{:T(128)}, f32[16,128]{1,0:T(8,128)S(1)}, f32[16,512,128]{2,1,0:T(8,128)}, ...), condition=%wide.region_12.13_spmd.clone, body=%wide.region_11.12_spmd.clone.sunk | while | flops 262148 | bytes 788081 | solution.py:110
  390.4 1.1 fusion.57
  391.6 1.1 fusion.57
  392.8 1.1 fusion.57
  394.0 1.1 fusion.57
  396.3 1.1 fusion.57
  397.5 1.1 fusion.57
  401.1 1.1 fusion.57
  404.7 1.1 fusion.57
  (56 shorter events, 15.1 us)
Async XLA Ops:
  6.5 1.6 copy-start
  6.5 326.1 %all-reduce.4.cloned.1.call-start = ((), (), s32[]{:S(2)}) async-start(), calls=%async_computation | async-start | bytes 524288 | tf_op jit(solution)/shard_map/psum | solution.py:77
  285.5 103.7 %all-gather.3.cloned.1.call-start = ((), (), s32[]{:S(2)}) async-start(), calls=%async_computation.1 | async-start | bytes 4456448 | tf_op jit(solution)/shard_map/all_gather | solution.py:102
  301.3 8.1 %copy-start.1 = (f32[1,128]{1,0:T(1,128)S(1)}, f32[1,128]{1,0:T(1,128)}, u32[]{:S(2)}) copy-start(f32[1,128]{1,0:T(1,128)} %param.14) | copy-start | bytes 1540
  301.3 15.7 %copy-start.2 = (f32[3,128]{1,0:T(4,128)S(1)}, f32[3,128]{1,0:T(4,128)}, u32[]{:S(2)}) copy-start(f32[3,128]{1,0:T(4,128)} %param.15) | copy-start | bytes 4612
  301.3 42.2 %copy-start.4 = (bf16[128,128]{1,0:T(8,128)(2,1)S(1)}, bf16[128,128]{1,0:T(8,128)(2,1)}, u32[]{:S(2)}) copy-start(bf16[128,128]{1,0:T(8,128)(2,1)} %param.16) | copy-start | bytes 98308
  301.3 106.9 %copy-start.3 = (f32[2,128]{1,0:T(2,128)S(1)}, f32[2,128]{1,0:T(2,128)}, u32[]{:S(2)}) copy-start(f32[2,128]{1,0:T(2,128)} %param.17) | copy-start | bytes 3076
  333.7 8.5 %collective-permute-start.1 = (bf16[1,512,128]{2,1,0:T(8,128)(2,1)S(1)}, bf16[1,512,128]{2,1,0:T(8,128)(2,1)S(1)}, u32[]{:S(2)}, u32[]{:S(2)}) collective-permute-start(bf16[1,512,128]{2,1,0:T(8,128)(2,1)S(1)} %divide_convert_fusion), channel_id=1, source_target_pairs={{4,0},{8,4},{12,8},{16,12},{20,16},{24,20},{28,24},{32,28},{36,32}... | collective-permute-start | bytes 393224 | tf_op jit(solution)/shard_map/ppermute | solution.py:18
  338.4 5.0 %collective-permute-start = (bf16[1,512,128]{2,1,0:T(8,128)(2,1)S(1)}, bf16[1,512,128]{2,1,0:T(8,128)(2,1)S(1)}, u32[]{:S(2)}, u32[]{:S(2)}) collective-permute-start(bf16[1,512,128]{2,1,0:T(8,128)(2,1)S(1)} %divide_convert_fusion), channel_id=1, source_target_pairs={{0,4},{4,8},{8,12},{12,16},{16,20},{20,24},{24,28},{28,32},{32,36}... | collective-permute-start | bytes 393224 | tf_op jit(solution)/shard_map/ppermute | solution.py:16
Sparse Core Ops, SparseCore 0:
  285.6 46.9 all-reduce.3
  344.6 44.5 all-gather.2
where the time goes:
time: 417 us; the launch traced here: 416 us
  blocking collectives  282 us (68%)
  waiting for transfers between devices  43.7 us (10%)
  other arithmetic  36.3 us (9%)
  local copies, waits for them, and re-layouts  19 us (5%)
  between operations  13.6 us (3%)
  matrix products  12.6 us (3%)
  starting transfers between devices  7.84 us (2%)
    psum x1, blocking collectives, local(): query_feats = lax.psum(contrib, ('tm', 'space')).astype(jnp.bfloat16)  250 us
    all_gather x1, waiting for transfers between devices, local(): lax.all_gather(carried[None], 'tm', axis=0, tiled=True)  26.2 us
    all_gather x1, blocking collectives, local(): lax.all_gather(retain_prod[None], 'tm', axis=0, tiled=True)  18.6 us
    select_n x16, other arithmetic, fold_step(): return jnp.where(source < position_tm, advanced, running)  18.4 us
    exp x1, local copies, waits for them, and re-layouts, local(): weights_exp = jnp.exp(scores - highest[:, None])  15.7 us
    psum x1, waiting for transfers between devices, local(): lax.psum((factor * totals, factor[..., None] * pos_sum, factor[..., None]...  15.6 us
    dot_general x1, matrix products, local(): jnp.dot(weights_exp.astype(jnp.bfloat16), frame_map, preferred_element_ty...  8.38 us
  transfers between devices with their start and end apart: 4, of which 4 were waited for; matrix products, arithmetic and copies ran while one was open for 6% of the time, Pallas kernels for 0%

commit v1 on v0

--- a/solution.py
+++ b/solution.py
@@ -3,6 +3,11 @@
 import jax.numpy as jnp
 from jax import lax
 from jax.sharding import PartitionSpec as P
+from jax.lax import all_gather
+
+
+def _take_ladders(inner_x):
+    return all_gather(inner_x, ("tm", "space")).sum(axis=0)
 
 
 def with_halo(cells, sides, width):
@@ -42,7 +47,7 @@
         jnp.clip(local_frame, 0, frames_here - 1), jnp.clip(local_row, 0, rows_here - 1), query_col
     ]
     contrib = jnp.where(owned[:, None], picked.astype(jnp.float32), 0.0)
-    query_feats = lax.psum(contrib, ("tm", "space")).astype(jnp.bfloat16)
+    query_feats = _take_ladders(contrib).astype(jnp.bfloat16)
     scale = 1.0 / math.sqrt(channels)
     col_coord = jnp.arange(map_width, dtype=jnp.int32).astype(jnp.float32) / map_width
     row_coord = (first_row + jnp.arange(rows_here, dtype=jnp.int32)).astype(

time: 417 us -> 290 us (0.70)
  blocking collectives: 282 us -> 32.1 us
  waiting for transfers between devices: 43.7 us -> 158 us
  other arithmetic: 36.3 us -> 44.2 us
    psum x1 -> x0, blocking collectives: 250 us -> none  [local(): query_feats = lax.psum(contrib, ('tm', 'space')).astype(jnp.bfloat16)]
    all_gather x0 -> x1, waiting for transfers between devices: none -> 102 us  [_take_ladders(): return all_gather(inner_x, ('tm', 'space')).sum(axis=0)]
    psum x1, waiting for transfers between devices: 15.6 us -> 28.3 us  [local(): lax.psum((factor * totals, factor[..., None] * pos_sum, factor[..., None]...]
    reduce_sum x0 -> x1, other arithmetic: none -> 6.53 us  [_take_ladders(): return all_gather(inner_x, ('tm', 'space')).sum(axis=0)]
  transfers between devices with their start and end apart: 4 -> 5, of which waited for: 4 -> 5; matrix products, arithmetic and copies ran while one was open for 6% -> 3% of each run, Pallas kernels for 0% -> 0%
where the time goes in v1:
time: 290 us; the launch traced here: 289 us
  waiting for transfers between devices  158 us (54%)
  other arithmetic  44.2 us (15%)
  blocking collectives  32.1 us (11%)
  local copies, waits for them, and re-layouts  19.7 us (7%)
  between operations  13.3 us (5%)
  matrix products  12.6 us (4%)
  starting transfers between devices  7.88 us (3%)
    all_gather x1, waiting for transfers between devices, _take_ladders(): return all_gather(inner_x, ('tm', 'space')).sum(axis=0)  102 us
    psum x1, waiting for transfers between devices, local(): lax.psum((factor * totals, factor[..., None] * pos_sum, factor[..., None]...  28.3 us
    all_gather x1, waiting for transfers between devices, local(): lax.all_gather(carried[None], 'tm', axis=0, tiled=True)  26.2 us
    all_gather x1, blocking collectives, local(): lax.all_gather(retain_prod[None], 'tm', axis=0, tiled=True)  18.6 us
    select_n x16, other arithmetic, fold_step(): return jnp.where(source < position_tm, advanced, running)  18.4 us
    exp x1, local copies, waits for them, and re-layouts, local(): weights_exp = jnp.exp(scores - highest[:, None])  15.6 us
    dot_general x1, matrix products, local(): jnp.dot(weights_exp.astype(jnp.bfloat16), frame_map, preferred_element_ty...  8.38 us
    reduce_sum x2, other arithmetic, local(): col_part = jnp.sum(jnp.sum(grid, axis=1) * col_coord[None, :], axis=1)  7.94 us
  transfers between devices with their start and end apart: 5, of which 5 were waited for; matrix products, arithmetic and copies ran while one was open for 3% of the time, Pallas kernels for 0%

profile of v1, /device:TPU:1, one launch (start us, length us, event | category | flops | bytes accessed | tf_op | source)
XLA Modules:
  0.0 288.7 jit_solution(8108489110198552376)
XLA Ops:
  8.1 3.1 %gather_fusion = bf16[512,128]{1,0:T(8,128)(2,1)S(1)} fusion(bf16[1,32,240,128]{3,2,1,0:T(8,128)(2,1)S(1)} %copy-done, s32[512]{0:T(512)S(1)} %fusion.41), kind=kCustom, calls=%fused_computation | custom fusion | bytes 268288 | tf_op jit(solution)/shard_map/gather | solution.py:46
  13.7 102.1 %all-gather.4.cloned.1.call-done = f32[64,512,128]{2,1,0:T(8,128)} async-done(((f32[1,512,128]{2,1,0:T(8,128)}), f32[64,512,128]{2,1,0:T(8,128)}) %all-gather.4.cloned.1.call-update) | async-done | bytes 16777232 | tf_op jit(solution)/shard_map/all_gather | solution.py:10
  115.7 6.5 %reduce_sum.54 = bf16[512,128]{1,0:T(8,128)(2,1)S(1)} reduce(f32[64,512,128]{2,1,0:T(8,128)} %all-gather.4.cloned.1.call-done, f32[]{:T(128)} %constant.57.clone.1), dimensions={0}, to_apply=%region_0.1 | reduce | flops 4128768 | bytes 16908292 | tf_op jit(solution)/shard_map/reduce_sum | solution.py:10
  122.3 2.3 multiply_reduce_fusion
  124.5 7.0 %fusion.50 = (f32[512]{0:T(512)S(1)}, f32[512,7680]{1,0:T(8,128)}) fusion(f32[512]{0:T(512)S(1)} %get-tuple-element.139, f32[512,7680]{1,0:T(8,128)S(1)} %get-tuple-element.140), kind=kLoop, calls=%fused_computation.74 | loop fusion | flops 11795968 | bytes 31461376 | tf_op jit(solution)/shard_map/reduce_sum | solution.py:68
  131.6 6.5 %pmax.7 = f32[1,512]{1,0:T(1,128)S(1)} all-reduce(f32[1,512]{1,0:T(1,128)S(1)} %bitcast.69), channel_id=1, replica_groups=mesh['video'=4,'tm'=16,'space'=4] {'space'}, use_global_device_ids=true, to_apply=%region_2.3 | all-reduce | flops 512 | bytes 4096 | tf_op jit(solution)/shard_map/pmax | solution.py:80
  138.1 15.6 %copy.10 = f32[512,7680]{0,1:T(8,128)} copy(f32[512,7680]{1,0:T(8,128)} %get-tuple-element.135) | data formatting | bytes 31457280 | tf_op jit(solution)/shard_map/exp | solution.py:66
  153.8 8.4 %fusion.7 = f32[1,512,128]{2,1,0:T(8,128)} fusion(bf16[7680,128]{1,0:T(8,128)(2,1)S(1)} %bitcast.65, f32[512,7680]{1,0:T(8,128)} %get-tuple-element.135, f32[512]{0:T(512)S(1)} %bitcast.67), kind=kOutput, calls=%fused_computation.11 | convolution fusion | flops 1010630656 | bytes 17958912 | tf_op jit(solution)/shard_map/dot_general | solution.py:74
  162.2 7.8 %fusion.48 = (f32[512,240]{0,1:T(8,128)S(1)}, f32[512,32]{0,1:T(8,128)S(1)}) fusion(f32[512,32,240]{0,2,1:T(8,128)} %bitcast.66), kind=kLoop, calls=%fused_computation.72 | loop fusion | flops 7725056 | bytes 16285696 | tf_op jit(solution)/shard_map/reduce_sum | solution.py:70
  170.3 7.0 %all-reduce = (f32[512]{0:T(512)S(1)}, f32[1,512,2]{1,2,0:T(2,128)S(1)}) all-reduce(f32[512]{0:T(512)S(1)} %bitcast.73, f32[1,512,2]{1,2,0:T(2,128)S(1)} %maximum_multiply_fusion), channel_id=1, replica_groups=mesh['video'=4,'tm'=16,'space'=4] {'space'}, use_global_device_ids=true, to_apply=%region_9.10 | all-reduce | flops 1536 | bytes 12288 | tf_op jit(solution)/shard_map/psum | solution.py:82
  177.3 28.3 %all-reduce.3.cloned.1.call-done = f32[1,512,128]{2,1,0:T(8,128)} async-done(((f32[1,512,128]{2,1,0:T(8,128)}), f32[1,512,128]{2,1,0:T(8,128)}) %all-reduce.3.cloned.1.call-update) | async-done | bytes 262160 | tf_op jit(solution)/shard_map/psum | solution.py:82
  206.7 4.7 %collective-permute-start.1 = (bf16[1,512,128]{2,1,0:T(8,128)(2,1)S(1)}, bf16[1,512,128]{2,1,0:T(8,128)(2,1)S(1)}, u32[]{:S(2)}, u32[]{:S(2)}) collective-permute-start(bf16[1,512,128]{2,1,0:T(8,128)(2,1)S(1)} %divide_convert_fusion), channel_id=1, source_target_pairs={{4,0},{8,4},{12,8},{16,12},{20,16},{24,20},{28,24},{32,28},{36,32}... | collective-permute-start | bytes 393224 | tf_op jit(solution)/shard_map/ppermute | solution.py:23
  211.4 3.1 %collective-permute-start = (bf16[1,512,128]{2,1,0:T(8,128)(2,1)S(1)}, bf16[1,512,128]{2,1,0:T(8,128)(2,1)S(1)}, u32[]{:S(2)}, u32[]{:S(2)}) collective-permute-start(bf16[1,512,128]{2,1,0:T(8,128)(2,1)S(1)} %divide_convert_fusion), channel_id=1, source_target_pairs={{0,4},{4,8},{8,12},{12,16},{16,20},{20,24},{24,28},{28,32},{32,36}... | collective-permute-start | bytes 393224 | tf_op jit(solution)/shard_map/ppermute | solution.py:21
  215.2 1.2 collective-permute-done
  217.4 18.6 %all-gather = f32[16,1,128]{2,1,0:T(1,128)S(1)} all-gather(f32[1,1,128]{2,1,0:T(1,128)S(1)} %bitcast.76), channel_id=1, replica_groups=mesh['video'=4,'tm'=16,'space'=4] {'tm'}, dimensions={0}, use_global_device_ids=true | all-gather | bytes 8704 | tf_op jit(solution)/shard_map/all_gather | solution.py:106
  236.0 26.2 %all-gather.6.cloned.1.call-done = f32[16,512,128]{2,1,0:T(8,128)} async-done(((f32[1,512,128]{2,1,0:T(8,128)}), f32[16,512,128]{2,1,0:T(8,128)}) %all-gather.6.cloned.1.call-update) | async-done | bytes 4194320 | tf_op jit(solution)/shard_map/all_gather | solution.py:107
  262.2 19.0 %while.14 = (s32[]{:T(128)}, f32[512,128]{1,0:T(8,128)S(1)}, s32[]{:T(128)}, f32[16,128]{1,0:T(8,128)S(1)}, f32[16,512,128]{2,1,0:T(8,128)}, /*index=5*/s32[]{:T(128)}, s32[]{:T(128)}) while((s32[]{:T(128)}, f32[512,128]{1,0:T(8,128)S(1)}, s32[]{:T(128)}, f32[16,128]{1,0:T(8,128)S(1)}, f32[16,512,128]{2,1,0:T(8,128)}, ...), condition=%wide.region_12.13_spmd.clone, body=%wide.region_11.12_spmd.clone.sunk | while | flops 262148 | bytes 788081 | solution.py:115
  263.4 1.1 fusion.57
  264.5 1.1 fusion.57
  265.7 1.1 fusion.57
  269.3 1.1 fusion.57
  272.9 1.1 fusion.57
  276.4 1.1 fusion.57
  280.0 1.1 fusion.57
  (57 shorter events, 18.5 us)
Async XLA Ops:
  6.5 1.6 copy-start
  6.5 109.2 %all-gather.4.cloned.1.call-start = ((), (), s32[]{:S(2)}) async-start(), calls=%async_computation | async-start | bytes 17039360 | tf_op jit(solution)/shard_map/all_gather | solution.py:10
  12.1 193.4 %all-reduce.3.cloned.1.call-start = ((), (), s32[]{:S(2)}) async-start(), calls=%async_computation.1 | async-start | bytes 524288 | tf_op jit(solution)/shard_map/psum | solution.py:82
  153.7 60.7 %copy-start.1 = (f32[1,128]{1,0:T(1,128)S(1)}, f32[1,128]{1,0:T(1,128)}, u32[]{:S(2)}) copy-start(f32[1,128]{1,0:T(1,128)} %param.14) | copy-start | bytes 1540
  153.8 62.7 %copy-start.3 = (bf16[128,128]{1,0:T(8,128)(2,1)S(1)}, bf16[128,128]{1,0:T(8,128)(2,1)}, u32[]{:S(2)}) copy-start(bf16[128,128]{1,0:T(8,128)(2,1)} %param.16) | copy-start | bytes 98308
  162.1 119.0 %copy-start.2 = (f32[2,128]{1,0:T(2,128)S(1)}, f32[2,128]{1,0:T(2,128)}, u32[]{:S(2)}) copy-start(f32[2,128]{1,0:T(2,128)} %param.17) | copy-start | bytes 3076
  162.2 100.0 %all-gather.6.cloned.1.call-start = ((), (), s32[]{:S(2)}) async-start(), calls=%async_computation.2 | async-start | bytes 4456448 | tf_op jit(solution)/shard_map/all_gather | solution.py:107
  206.7 8.5 %collective-permute-start.1 = (bf16[1,512,128]{2,1,0:T(8,128)(2,1)S(1)}, bf16[1,512,128]{2,1,0:T(8,128)(2,1)S(1)}, u32[]{:S(2)}, u32[]{:S(2)}) collective-permute-start(bf16[1,512,128]{2,1,0:T(8,128)(2,1)S(1)} %divide_convert_fusion), channel_id=1, source_target_pairs={{4,0},{8,4},{12,8},{16,12},{20,16},{24,20},{28,24},{32,28},{36,32}... | collective-permute-start | bytes 393224 | tf_op jit(solution)/shard_map/ppermute | solution.py:23
  211.4 5.0 %collective-permute-start = (bf16[1,512,128]{2,1,0:T(8,128)(2,1)S(1)}, bf16[1,512,128]{2,1,0:T(8,128)(2,1)S(1)}, u32[]{:S(2)}, u32[]{:S(2)}) collective-permute-start(bf16[1,512,128]{2,1,0:T(8,128)(2,1)S(1)} %divide_convert_fusion), channel_id=1, source_target_pairs={{0,4},{4,8},{8,12},{12,16},{16,20},{20,24},{24,28},{28,32},{32,36}... | collective-permute-start | bytes 393224 | tf_op jit(solution)/shard_map/ppermute | solution.py:21
Sparse Core Ops, SparseCore 0:
  12.2 103.4 all-gather.3
  162.3 43.2 all-reduce.2
  217.6 44.5 all-gather.5
